TPU v7x, 128 devices: a whole 4x4x4 slice. The times are simulated.
128 devices in a mesh: grp: 32 (over z, x_hi, y), head: 4 (over x_lo, core).
Axes of the slice: x: 4 (x_hi: 2, x_lo: 2; x = x_hi * 2 + x_lo), y: 4, z: 4, core: 2. Of those that a mesh axis runs over, the one named last changes fastest.
Arguments:
- hidden_in: bfloat16 [32, 128, 2048], P('grp'), may hold values from -6 to 6
- attn_gain: float32 [2048], replicated, may hold values from 0.1 to 1.9
- w_query: bfloat16 [2048, 2048], P(None, 'head'), may hold values from -0.125 to 0.125
- w_key: bfloat16 [2048, 2048], P(None, 'head'), may hold values from -0.125 to 0.125
- w_value: bfloat16 [2048, 2048], P(None, 'head'), may hold values from -0.125 to 0.125
- w_out: bfloat16 [2048, 2048], P('head'), may hold values from -0.125 to 0.125
- cache: bfloat16 [2, 32, 4096, 2048], P(None, None, 'grp', 'head'), may hold values from -900 to 900
- prefix_len: int32 [32], replicated, may hold values from 1 to 4096, 65536 in all
- mlp_gain: float32 [2048], replicated, may hold values from 0.1 to 1.9
- expert_ids: int32 [32, 128, 8], P('grp'), may hold values from 0 to 63, all different within a row; in each aligned block of 128 rows (0 to 127, 128 to 255, ..., all dimensions but the last counted through in order) at most 24 rows name the same one
- route_weight: float32 [32, 128, 8], P('grp'), may hold values from 0.05 to 1
- w_gate: bfloat16 [64, 2048, 1024], P('grp', None, 'head'), may hold values from -0.125 to 0.125
- w_up: bfloat16 [64, 2048, 1024], P('grp', None, 'head'), may hold values from -0.125 to 0.125
- w_down: bfloat16 [64, 1024, 2048], P('grp', 'head'), may hold values from -0.1875 to 0.1875
Outputs:
- layer_out: bfloat16 [32, 128, 2048], P('grp', None, 'head')
Inputs may be any that keep to these rules, and one draw needn't show every extreme that they name: `expert_ids`: among one prompt's 128 tokens no expert is chosen more than 24 times; a token's 8 experts are distinct.
All inputs are finite; a program needn't handle non-finite values.
Results may differ from a plain program's by a relative error of at most 0.017.
The roundings to bfloat16 on the way count: a program that leaves them out, or rounds other values in their place, can miss the bound.
Values may be sent and summed in bfloat16 or wider, within the bound.
A program may use at most 128 MiB of HBM per device.

v0:
```python
import jax
import jax.numpy as jnp
from jax import lax
from jax.sharding import PartitionSpec as P

HD = 128
TOPK = 8


def rms_norm(values, gain):
    scale = lax.rsqrt(jnp.mean(values * values, axis=-1, keepdims=True) + 1e-05)
    return values * scale * gain


def rotate(tensor, position):
    half = HD // 2
    inverse = 10000.0 ** (-(jnp.arange(half).astype(jnp.float32) * 2.0) / HD)
    angle = position[:, None] * inverse[None, :]
    cosine = jnp.cos(angle)[:, None, :]
    sine = jnp.sin(angle)[:, None, :]
    first = tensor[..., :half]
    second = tensor[..., half:]
    return jnp.concatenate(
        [first * cosine - second * sine, second * cosine + first * sine], axis=-1
    )


def on_device(
    hidden_in,
    attn_gain,
    w_query,
    w_key,
    w_value,
    w_out,
    cache,
    prefix_len,
    mlp_gain,
    expert_ids,
    route_weight,
    w_gate,
    w_up,
    w_down,
):
    group_count = lax.axis_size("grp")
    head_count = lax.axis_size("head")
    my_prompt = lax.axis_index("grp")
    tokens = hidden_in.shape[1]
    width = hidden_in.shape[2]
    heads_here = w_query.shape[1] // HD
    length = prefix_len[my_prompt]
    rows = hidden_in[0].astype(jnp.float32)
    normed = rms_norm(rows, attn_gain).astype(jnp.bfloat16)
    position = (length + jnp.arange(tokens)).astype(jnp.float32)
    query = jnp.dot(normed, w_query, preferred_element_type=jnp.float32).reshape(
        tokens, heads_here, HD
    )
    key_new = jnp.dot(normed, w_key, preferred_element_type=jnp.float32).reshape(
        tokens, heads_here, HD
    )
    value_new = jnp.dot(normed, w_value, preferred_element_type=jnp.float32).reshape(
        tokens, heads_here, HD
    )
    query = (rotate(query, position) * HD ** (-0.5)).astype(jnp.bfloat16)
    key_new = rotate(key_new, position).astype(jnp.bfloat16)
    value_new = value_new.astype(jnp.bfloat16)
    relaid = lax.all_to_all(cache, "grp", split_axis=1, concat_axis=2, tiled=True)
    context = relaid.shape[2]
    cache_key = relaid[0, 0].reshape(context, heads_here, HD)
    cache_value = relaid[1, 0].reshape(context, heads_here, HD)
    score_old = jnp.einsum("qhd,khd->hqk", query, cache_key, preferred_element_type=jnp.float32)
    score_new = jnp.einsum("qhd,khd->hqk", query, key_new, preferred_element_type=jnp.float32)
    allow_old = (jnp.arange(context) < length)[None, None, :]
    allow_new = (jnp.arange(tokens)[None, :] <= jnp.arange(tokens)[:, None])[None, :, :]
    score_old = jnp.where(allow_old, score_old, -1e30)
    score_new = jnp.where(allow_new, score_new, -1e30)
    top = jnp.maximum(
        jnp.max(score_old, axis=-1, keepdims=True), jnp.max(score_new, axis=-1, keepdims=True)
    )
    prob_old = jnp.where(allow_old, jnp.exp(score_old - top), 0.0)
    prob_new = jnp.where(allow_new, jnp.exp(score_new - top), 0.0)
    total = jnp.sum(prob_old, axis=-1) + jnp.sum(prob_new, axis=-1)
    numer = jnp.einsum(
        "hqk,khd->qhd",
        prob_old.astype(jnp.bfloat16),
        cache_value,
        preferred_element_type=jnp.float32,
    )
    numer = numer + jnp.einsum(
        "hqk,khd->qhd", prob_new.astype(jnp.bfloat16), value_new, preferred_element_type=jnp.float32
    )
    attended = (
        (numer / jnp.transpose(total)[:, :, None])
        .reshape(tokens, heads_here * HD)
        .astype(jnp.bfloat16)
    )
    projected = jnp.dot(attended, w_out, preferred_element_type=jnp.float32)
    resid = rows + lax.psum(projected.astype(jnp.bfloat16), "head").astype(jnp.float32)
    mixed_in = rms_norm(resid, mlp_gain).astype(jnp.bfloat16)
    experts_here = w_gate.shape[0]
    expert_total = experts_here * group_count
    capacity = max(2, 3 * tokens * TOPK // (2 * expert_total))
    chosen = expert_ids[0].reshape(tokens * TOPK)
    weights = route_weight[0]
    one_hot = (chosen[:, None] == jnp.arange(expert_total)[None, :]).astype(jnp.int32)
    before = jnp.cumsum(one_hot, axis=0) - one_hot
    slot = jnp.sum(before * one_hot, axis=1)
    target = chosen * capacity + slot
    repeated = jnp.repeat(mixed_in, TOPK, axis=0)
    outgoing = jnp.zeros((expert_total * capacity, width), jnp.bfloat16).at[target].set(repeated)
    outgoing = outgoing.reshape(group_count, experts_here, capacity, width)
    arrived = lax.all_to_all(outgoing, "grp", split_axis=0, concat_axis=0, tiled=True)
    results = []
    for expert in range(experts_here):
        inputs = arrived[:, expert].reshape(group_count * capacity, width)
        gate = jnp.dot(inputs, w_gate[expert], preferred_element_type=jnp.float32)
        upper = jnp.dot(inputs, w_up[expert], preferred_element_type=jnp.float32)
        act = (jax.nn.silu(gate) * upper).astype(jnp.bfloat16)
        output = jnp.dot(act, w_down[expert], preferred_element_type=jnp.float32).astype(
            jnp.bfloat16
        )
        results.append(output.reshape(group_count, capacity, width))
    expert_out = jnp.stack(results, axis=1)
    share_width = width // head_count
    returned = lax.all_to_all(expert_out, "grp", split_axis=0, concat_axis=0, tiled=True)
    returned = returned.reshape(expert_total * capacity, width)
    picked = returned[target].reshape(tokens, TOPK, width)
    combined = jnp.einsum("tk,tkd->td", weights, picked.astype(jnp.float32))
    moe_share = lax.psum_scatter(
        combined.astype(jnp.bfloat16), "head", scatter_dimension=1, tiled=True
    ).astype(jnp.float32)
    resid_share = lax.dynamic_slice_in_dim(
        resid, lax.axis_index("head") * share_width, share_width, 1
    )
    return (resid_share + moe_share).astype(jnp.bfloat16)[None]


def solution(mesh):
    placed = (
        P("grp", None, None),
        P(),
        P(None, "head"),
        P(None, "head"),
        P(None, "head"),
        P("head", None),
        P(None, None, "grp", "head"),
        P(),
        P(),
        P("grp", None, None),
        P("grp", None, None),
        P("grp", None, "head"),
        P("grp", None, "head"),
        P("grp", "head", None),
    )
    return jax.shard_map(
        on_device, mesh=mesh, in_specs=placed, out_specs=P("grp", None, "head"), check_vma=False
    )
```

profile of v0, /device:TPU:1, one launch (start us, length us, event | category | flops | bytes accessed | tf_op | source)
XLA Modules:
  0.0 487.7 jit_solution(10138498314555336373)
XLA Ops:
  6.5 7.7 %copy.39 = bf16[2,32,128,512]{3,2,0,1:T(8,128)(2,1)} copy(bf16[2,32,128,512]{3,2,1,0:T(8,128)(2,1)} %param.20) | data formatting | bytes 16777216 | tf_op args[6]
  14.3 11.6 %all-to-all-start = ((bf16[2,32,128,512]{3,2,0,1:T(8,128)(2,1)}), bf16[2,32,128,512]{3,2,0,1:T(8,128)(2,1)}, u32[]{:S(2)}, u32[]{:S(2)}) async-start(bf16[2,32,128,512]{3,2,0,1:T(8,128)(2,1)} %copy.39), calls=%async_computation | async-start | bytes 16777216 | tf_op jit(solution)/shard_map/all_to_all | solution.py:66
  26.5 18.0 %reduce-window.6 = s32[64,8,128]{2,1,0:T(8,128)S(1)} reduce-window(s32[64,8,128]{2,1,0:T(8,128)S(1)} %fusion.67, s32[]{:T(128)} %constant.22.clone.1), window={size=1x1x128 pad=0_0x0_0x127_0}, to_apply=%region_6.7 | reduce-window | flops 8323072 | bytes 524292 | tf_op jit(solution)/shard_map/reduce-window
  44.9 4.0 copy.69
  48.9 4.0 copy.65
  52.9 4.0 copy.71
  64.3 73.1 %all-to-all-done = bf16[2,32,128,512]{3,2,0,1:T(8,128)(2,1)} async-done(((bf16[2,32,128,512]{3,2,0,1:T(8,128)(2,1)}), bf16[2,32,128,512]{3,2,0,1:T(8,128)(2,1)}, u32[]{:S(2)}, u32[]{:S(2)}) %all-to-all-start) | async-done | bytes 8388640 | tf_op jit(solution)/shard_map/all_to_all | solution.py:66
  137.4 5.9 %fusion.96 = (bf16[1,32,128,512]{3,2,0,1:T(8,128)(2,1)}, bf16[1,32,128,512]{3,2,0,1:T(8,128)(2,1)}) fusion(bf16[2,32,128,512]{3,2,0,1:T(8,128)(2,1)} %all-to-all-done), kind=kLoop, calls=%fused_computation.121 | loop fusion | bytes 16777216 | tf_op jit(solution)/shard_map/slice | solution.py:68
  143.3 6.9 %reshape.243 = bf16[4096,4,128]{2,1,0:T(4,128)(2,1)} reshape(bf16[1,32,128,512]{3,2,0,1:T(8,128)(2,1)} %get-tuple-element.6) | data formatting | bytes 8388608 | tf_op jit(solution)/shard_map/reshape;squeeze | solution.py:69
  150.2 6.9 %reshape.242 = bf16[4096,4,128]{2,1,0:T(4,128)(2,1)} reshape(bf16[1,32,128,512]{3,2,0,1:T(8,128)(2,1)} %get-tuple-element.5) | data formatting | bytes 8388608 | tf_op jit(solution)/shard_map/reshape;squeeze | solution.py:68
  157.1 3.8 select_reduce_fusion
  163.2 3.4 fusion.23
  166.7 2.6 fusion.28
  170.9 52.3 %all-reduce.2.cloned.1.call-done = bf16[128,2048]{1,0:T(8,128)(2,1)} async-done(((bf16[128,2048]{1,0:T(8,128)(2,1)}), bf16[128,2048]{1,0:T(8,128)(2,1)}) %all-reduce.2.cloned.1.call-update) | async-done | bytes 524304 | tf_op jit(solution)/shard_map/psum | solution.py:97
  226.7 10.4 %scatter_custom_fusion = bf16[1536,2048]{1,0:T(8,128)(2,1)} fusion(s32[1024]{0:T(1024)S(1)} %bitcast.138, bf16[]{:T(256)} %constant.49.clone.1, bf16[128,2048]{1,0:T(8,128)(2,1)S(1)} %multiply_convert_fusion), kind=kCustom, calls=%fused_computation.10 | custom fusion | bytes 6815746 | tf_op jit(solution)/shard_map/scatter | solution.py:109
  237.1 82.5 %all_to_all.19 = bf16[32,2,24,2048]{3,2,1,0:T(8,128)(2,1)S(1)} all-to-all(bf16[32,2,24,2048]{3,2,1,0:T(8,128)(2,1)} %bitcast.120), channel_id=1, replica_groups=mesh['grp'=32,'head'=4] {'grp'}, dimensions={0} | all-to-all | bytes 12582912 | tf_op jit(solution)/shard_map/all_to_all | solution.py:111
  325.3 7.9 %convolution_convert_fusion = bf16[768,2048]{1,0:T(8,128)(2,1)} fusion(bf16[768,2048]{1,0:T(8,128)(2,1)} %bitcast.126, bf16[2,256,2048]{2,1,0:T(8,128)(2,1)} %param.27, bf16[2,2048,256]{2,1,0:T(8,128)(2,1)} %param.26, f32[768,256]{1,0:T(8,128)} %fusion.35), kind=kOutput, calls=%fused_computation.19 | convolution fusion | flops 1613365248 | bytes 9175040 | tf_op jit(solution)/shard_map/dot_general | solution.py:118
  333.2 7.1 %convolution_convert_fusion.1 = bf16[768,2048]{1,0:T(8,128)(2,1)} fusion(bf16[768,2048]{1,0:T(8,128)(2,1)} %bitcast.124, bf16[2,256,2048]{2,1,0:T(8,128)(2,1)S(1)} %copy-done.11, bf16[2,2048,256]{2,1,0:T(8,128)(2,1)} %param.26, f32[768,256]{1,0:T(8,128)S(1)} %fusion.40), kind=kOutput, calls=%fused_computation.20 | convolution fusion | flops 1613365248 | bytes 9175040 | tf_op jit(solution)/shard_map/dot_general | solution.py:118
  340.3 6.1 %pad_maximum_fusion = bf16[32,2,24,2048]{3,2,1,0:T(8,128)(2,1)} fusion(bf16[32,1,24,2048]{3,2,1,0:T(8,128)(2,1)} %bitcast.127, bf16[32,1,24,2048]{3,2,1,0:T(8,128)(2,1)} %bitcast.128), kind=kLoop, calls=%fused_computation.6 | loop fusion | flops 3145728 | bytes 12582912 | tf_op jit(solution)/shard_map/stack | solution.py:122
  346.4 7.3 %all-to-all-start.2 = ((bf16[32,2,24,2048]{3,2,1,0:T(8,128)(2,1)}), bf16[32,2,24,2048]{3,2,1,0:T(8,128)(2,1)}, u32[]{:S(2)}, u32[]{:S(2)}) async-start(bf16[32,2,24,2048]{3,2,1,0:T(8,128)(2,1)} %pad_maximum_fusion), calls=%async_computation.2 | async-start | bytes 12582912 | tf_op jit(solution)/shard_map/all_to_all | solution.py:124
  354.0 87.2 %all-to-all-done.2 = bf16[32,2,24,2048]{3,2,1,0:T(8,128)(2,1)} async-done(((bf16[32,2,24,2048]{3,2,1,0:T(8,128)(2,1)}), bf16[32,2,24,2048]{3,2,1,0:T(8,128)(2,1)}, u32[]{:S(2)}, u32[]{:S(2)}) %all-to-all-start.2) | async-done | bytes 6291488 | tf_op jit(solution)/shard_map/all_to_all | solution.py:124
  441.1 12.8 %gather_fusion = bf16[1024,2048]{1,0:T(8,128)(2,1)} fusion(bf16[1536,2048]{1,0:T(8,128)(2,1)} %bitcast.32, s32[1024]{0:T(1024)S(1)} %broadcast_clamp_fusion), kind=kCustom, calls=%fused_computation | custom fusion | bytes 8392704 | tf_op jit(solution)/shard_map/gather | solution.py:126
  453.9 3.4 fusion.4
  458.5 20.7 %reduce-scatter.2.cloned.1.call-done = bf16[128,512]{1,0:T(8,128)(2,1)} async-done(((bf16[128,2048]{1,0:T(8,128)(2,1)}), bf16[128,512]{1,0:T(8,128)(2,1)}) %reduce-scatter.2.cloned.1.call-update) | async-done | bytes 131088 | tf_op jit(solution)/shard_map/reduce_scatter | solution.py:128
  (72 shorter events, 24.3 us)
Async XLA Ops:
  6.5 162.8 %copy-start = (bf16[512,2048]{1,0:T(8,128)(2,1)S(1)}, bf16[512,2048]{1,0:T(8,128)(2,1)}, u32[]{:S(2)}) copy-start(bf16[512,2048]{1,0:T(8,128)(2,1)} %param.19) | copy-start | bytes 6291460
  14.3 11.7 %copy-start.7 = (s32[1,128,8]{1,2,0:T(8,128)S(1)}, s32[1,128,8]{1,2,0:T(8,128)}, u32[]{:S(2)}) copy-start(s32[1,128,8]{1,2,0:T(8,128)} %param.23) | copy-start | bytes 12292
  14.3 123.1 %all-to-all-start = ((bf16[2,32,128,512]{3,2,0,1:T(8,128)(2,1)}), bf16[2,32,128,512]{3,2,0,1:T(8,128)(2,1)}, u32[]{:S(2)}, u32[]{:S(2)}) async-start(bf16[2,32,128,512]{3,2,0,1:T(8,128)(2,1)} %copy.39), calls=%async_computation | async-start | bytes 16777216 | tf_op jit(solution)/shard_map/all_to_all | solution.py:66
  25.9 197.3 %all-reduce.2.cloned.1.call-start = ((), (), s32[]{:S(2)}) async-start(), calls=%async_computation.4 | async-start | bytes 1048576 | tf_op jit(solution)/shard_map/psum | solution.py:97
  48.9 8.0 %copy-start.12 = (s32[32]{0:T(128)S(1)}, s32[32]{0:T(128)}, u32[]{:S(2)}) copy-start(s32[32]{0:T(128)} %param.21) | copy-start | bytes 388
  48.9 9.9 %copy-start.2 = (bf16[1,128,2048]{2,1,0:T(8,128)(2,1)S(1)}, bf16[1,128,2048]{2,1,0:T(8,128)(2,1)}, u32[]{:S(2)}) copy-start(bf16[1,128,2048]{2,1,0:T(8,128)(2,1)} %param.14) | copy-start | bytes 1572868
  48.9 10.4 %copy-start.6 = (f32[2048]{0:T(1024)S(1)}, f32[2048]{0:T(1024)}, u32[]{:S(2)}) copy-start(f32[2048]{0:T(1024)} %param.15) | copy-start | bytes 24580
  160.9 2.2 copy-start.3
  166.7 58.8 %copy-start.8 = (f32[2048]{0:T(1024)S(1)}, f32[2048]{0:T(1024)}, u32[]{:S(2)}) copy-start(f32[2048]{0:T(1024)} %param.22) | copy-start | bytes 24580
  319.6 2.8 copy-start.10
  320.7 1.7 copy-start.5
  320.7 3.6 copy-start.4
  325.3 7.9 %copy-start.11 = (bf16[2,256,2048]{2,1,0:T(8,128)(2,1)S(1)}, bf16[2,256,2048]{2,1,0:T(8,128)(2,1)}, u32[]{:S(2)}) copy-start(bf16[2,256,2048]{2,1,0:T(8,128)(2,1)} %param.27) | copy-start | bytes 6291460
  346.4 7.4 %copy-start.9 = (f32[1,128,8]{1,2,0:T(8,128)S(1)}, f32[1,128,8]{1,2,0:T(8,128)}, u32[]{:S(2)}) copy-start(f32[1,128,8]{1,2,0:T(8,128)} %param.24) | copy-start | bytes 12292
  346.4 94.7 %all-to-all-start.2 = ((bf16[32,2,24,2048]{3,2,1,0:T(8,128)(2,1)}), bf16[32,2,24,2048]{3,2,1,0:T(8,128)(2,1)}, u32[]{:S(2)}, u32[]{:S(2)}) async-start(bf16[32,2,24,2048]{3,2,1,0:T(8,128)(2,1)} %pad_maximum_fusion), calls=%async_computation.2 | async-start | bytes 12582912 | tf_op jit(solution)/shard_map/all_to_all | solution.py:124
  353.7 125.5 %reduce-scatter.2.cloned.1.call-start = ((), (), s32[]{:S(2)}) async-start(), calls=%async_computation.5 | async-start | bytes 655360 | tf_op jit(solution)/shard_map/reduce_scatter | solution.py:128
  441.1 39.8 %copy-start.1 = (bf16[512,2048]{1,0:T(8,128)(2,1)S(1)}, bf16[512,2048]{1,0:T(8,128)(2,1)}, u32[]{:S(2)}) copy-start(bf16[512,2048]{1,0:T(8,128)(2,1)} %param.19) | copy-start | bytes 6291460
Sparse Core Ops, SparseCore 0:
  170.8 52.3 all-reduce.1
  458.6 20.5 reduce-scatter.1
where the time goes:
time: 489 us; the launch traced here: 488 us
  waiting for transfers between devices  233 us (48%)
  blocking collectives  82.5 us (17%)
  local copies, waits for them, and re-layouts  68.1 us (14%)
  matrix products  37.4 us (8%)
  other arithmetic  33.7 us (7%)
  starting transfers between devices  19 us (4%)
  between operations  13.7 us (3%)
    all_to_all x1, waiting for transfers between devices, on_device(): lax.all_to_all(expert_out, 'grp', split_axis=0, concat_axis=0, tiled=True)  87.2 us
    all_to_all x1, blocking collectives, on_device(): lax.all_to_all(outgoing, 'grp', split_axis=0, concat_axis=0, tiled=True)  82.5 us
    all_to_all x1, waiting for transfers between devices, on_device(): lax.all_to_all(cache, 'grp', split_axis=1, concat_axis=2, tiled=True)  73.1 us
    psum x1, waiting for transfers between devices, on_device(): lax.psum(projected.astype(jnp.bfloat16), 'head').astype(jnp.float32)  52.3 us
    reduce_scatter x1, waiting for transfers between devices, on_device(): lax.psum_scatter(combined.astype(jnp.bfloat16), 'head', scatter_dimension...  20.7 us
    another operation x4, other arithmetic  18.2 us
    dot_general x2, matrix products, on_device(): jnp.dot(act, w_down[expert], preferred_element_type=jnp.float32)  15 us
    gather x1, local copies, waits for them, and re-layouts, on_device(): picked = returned[target].reshape(tokens, TOPK, width)  12.8 us
  transfers between devices with their start and end apart: 4, of which 4 were waited for; matrix products, arithmetic and copies ran while one was open for 8% of the time, Pallas kernels for 0%

commit v1 on v0

--- a/solution.py
+++ b/solution.py
@@ -94,7 +94,9 @@
         .astype(jnp.bfloat16)
     )
     projected = jnp.dot(attended, w_out, preferred_element_type=jnp.float32)
-    resid = rows + lax.psum(projected.astype(jnp.bfloat16), "head").astype(jnp.float32)
+    resid = rows + jnp.sum(lax.all_gather(projected.astype(jnp.bfloat16), "head"), axis=0).astype(
+        jnp.float32
+    )
     mixed_in = rms_norm(resid, mlp_gain).astype(jnp.bfloat16)
     experts_here = w_gate.shape[0]
     expert_total = experts_here * group_count

time: 489 us -> 478 us (0.978)
  waiting for transfers between devices: 233 us -> 224 us
    psum x1 -> x0, waiting for transfers between devices: 52.3 us -> none  [on_device(): lax.psum(projected.astype(jnp.bfloat16), 'head').astype(jnp.float32)]
    all_gather x0 -> x1, waiting for transfers between devices: none -> 24.8 us  [on_device(): lax.all_gather(projected.astype(jnp.bfloat16), 'head')]
    all_to_all x1, waiting for transfers between devices: 73.1 us -> 92 us  [on_device(): lax.all_to_all(cache, 'grp', split_axis=1, concat_axis=2, tiled=True)]
where the time goes in v1:
time: 478 us; the launch traced here: 477 us
  waiting for transfers between devices  224 us (47%)
  blocking collectives  82.6 us (17%)
  local copies, waits for them, and re-layouts  68.1 us (14%)
  matrix products  35.5 us (7%)
  other arithmetic  33.6 us (7%)
  starting transfers between devices  19 us (4%)
  between operations  13.7 us (3%)
    all_to_all x1, waiting for transfers between devices, on_device(): lax.all_to_all(cache, 'grp', split_axis=1, concat_axis=2, tiled=True)  92 us
    all_to_all x1, waiting for transfers between devices, on_device(): lax.all_to_all(expert_out, 'grp', split_axis=0, concat_axis=0, tiled=True)  83.2 us
    all_to_all x1, blocking collectives, on_device(): lax.all_to_all(outgoing, 'grp', split_axis=0, concat_axis=0, tiled=True)  82.6 us
    all_gather x1, waiting for transfers between devices, on_device(): lax.all_gather(projected.astype(jnp.bfloat16), 'head')  24.8 us
    reduce_scatter x1, waiting for transfers between devices, on_device(): lax.psum_scatter(combined.astype(jnp.bfloat16), 'head', scatter_dimension...  24.1 us
    another operation x4, other arithmetic  18.2 us
    dot_general x2, matrix products, on_device(): jnp.dot(act, w_down[expert], preferred_element_type=jnp.float32)  15 us
    gather x1, local copies, waits for them, and re-layouts, on_device(): picked = returned[target].reshape(tokens, TOPK, width)  12.8 us
  transfers between devices with their start and end apart: 4, of which 4 were waited for; matrix products, arithmetic and copies ran while one was open for 8% of the time, Pallas kernels for 0%

profile of v1, /device:TPU:1, one launch (start us, length us, event | category | flops | bytes accessed | tf_op | source)
XLA Modules:
  0.0 476.7 jit_solution(10455435979040509885)
XLA Ops:
  6.5 7.7 %copy.39 = bf16[2,32,128,512]{3,2,0,1:T(8,128)(2,1)} copy(bf16[2,32,128,512]{3,2,1,0:T(8,128)(2,1)} %param.20) | data formatting | bytes 16777216 | tf_op args[6]
  14.3 11.5 %all-to-all-start = ((bf16[2,32,128,512]{3,2,0,1:T(8,128)(2,1)}), bf16[2,32,128,512]{3,2,0,1:T(8,128)(2,1)}, u32[]{:S(2)}, u32[]{:S(2)}) async-start(bf16[2,32,128,512]{3,2,0,1:T(8,128)(2,1)} %copy.39), calls=%async_computation | async-start | bytes 16777216 | tf_op jit(solution)/shard_map/all_to_all | solution.py:66
  25.8 4.0 copy.69
  29.8 4.0 copy.65
  33.8 4.0 copy.71
  45.2 92.0 %all-to-all-done = bf16[2,32,128,512]{3,2,0,1:T(8,128)(2,1)} async-done(((bf16[2,32,128,512]{3,2,0,1:T(8,128)(2,1)}), bf16[2,32,128,512]{3,2,0,1:T(8,128)(2,1)}, u32[]{:S(2)}, u32[]{:S(2)}) %all-to-all-start) | async-done | bytes 8388640 | tf_op jit(solution)/shard_map/all_to_all | solution.py:66
  137.3 5.9 %fusion.96 = (bf16[1,32,128,512]{3,2,0,1:T(8,128)(2,1)}, bf16[1,32,128,512]{3,2,0,1:T(8,128)(2,1)}) fusion(bf16[2,32,128,512]{3,2,0,1:T(8,128)(2,1)} %all-to-all-done), kind=kLoop, calls=%fused_computation.121 | loop fusion | bytes 16777216 | tf_op jit(solution)/shard_map/slice | solution.py:68
  143.2 6.9 %reshape.244 = bf16[4096,4,128]{2,1,0:T(4,128)(2,1)} reshape(bf16[1,32,128,512]{3,2,0,1:T(8,128)(2,1)} %get-tuple-element.6) | data formatting | bytes 8388608 | tf_op jit(solution)/shard_map/reshape;squeeze | solution.py:69
  150.1 6.9 %reshape.243 = bf16[4096,4,128]{2,1,0:T(4,128)(2,1)} reshape(bf16[1,32,128,512]{3,2,0,1:T(8,128)(2,1)} %get-tuple-element.5) | data formatting | bytes 8388608 | tf_op jit(solution)/shard_map/reshape;squeeze | solution.py:68
  157.0 3.8 select_reduce_fusion
  163.0 2.4 fusion.23
  165.6 2.6 fusion.28
  170.0 18.0 %reduce-window.6 = s32[64,8,128]{2,1,0:T(8,128)S(1)} reduce-window(s32[64,8,128]{2,1,0:T(8,128)S(1)} %fusion.67, s32[]{:T(128)} %constant.22.clone.1), window={size=1x1x128 pad=0_0x0_0x127_0}, to_apply=%region_6.7 | reduce-window | flops 8323072 | bytes 524292 | tf_op jit(solution)/shard_map/reduce-window
  188.7 24.8 %all-gather.3.cloned.1.call-done = bf16[512,2048]{1,0:T(8,128)(2,1)} async-done(((bf16[128,2048]{1,0:T(8,128)(2,1)}), bf16[512,2048]{1,0:T(8,128)(2,1)}) %all-gather.3.cloned.1.call-update) | async-done | bytes 2097168 | tf_op jit(solution)/shard_map/all_gather | solution.py:97
  217.0 10.4 %scatter_custom_fusion = bf16[1536,2048]{1,0:T(8,128)(2,1)} fusion(s32[1024]{0:T(1024)S(1)} %bitcast.140, bf16[]{:T(256)} %constant.47.clone.1, bf16[128,2048]{1,0:T(8,128)(2,1)S(1)} %multiply_convert_fusion), kind=kCustom, calls=%fused_computation.10 | custom fusion | bytes 6815746 | tf_op jit(solution)/shard_map/scatter | solution.py:111
  227.4 82.6 %all_to_all.19 = bf16[32,2,24,2048]{3,2,1,0:T(8,128)(2,1)S(1)} all-to-all(bf16[32,2,24,2048]{3,2,1,0:T(8,128)(2,1)} %bitcast.121), channel_id=1, replica_groups=mesh['grp'=32,'head'=4] {'grp'}, dimensions={0} | all-to-all | bytes 12582912 | tf_op jit(solution)/shard_map/all_to_all | solution.py:113
  314.8 7.5 %convolution_convert_fusion = bf16[768,2048]{1,0:T(8,128)(2,1)} fusion(bf16[768,2048]{1,0:T(8,128)(2,1)} %bitcast.127, bf16[2,256,2048]{2,1,0:T(8,128)(2,1)} %param.27, bf16[2,2048,256]{2,1,0:T(8,128)(2,1)} %param.26, f32[768,256]{1,0:T(8,128)S(1)} %fusion.35), kind=kOutput, calls=%fused_computation.19 | convolution fusion | flops 1613365248 | bytes 9175040 | tf_op jit(solution)/shard_map/dot_general | solution.py:120
  322.3 7.4 %convolution_convert_fusion.1 = bf16[768,2048]{1,0:T(8,128)(2,1)} fusion(bf16[768,2048]{1,0:T(8,128)(2,1)} %bitcast.125, bf16[2,256,2048]{2,1,0:T(8,128)(2,1)} %param.27, bf16[2,2048,256]{2,1,0:T(8,128)(2,1)} %param.26, f32[768,256]{1,0:T(8,128)S(1)} %fusion.40), kind=kOutput, calls=%fused_computation.20 | convolution fusion | flops 1613365248 | bytes 9175040 | tf_op jit(solution)/shard_map/dot_general | solution.py:120
  329.8 6.1 %pad_maximum_fusion = bf16[32,2,24,2048]{3,2,1,0:T(8,128)(2,1)} fusion(bf16[32,1,24,2048]{3,2,1,0:T(8,128)(2,1)} %bitcast.128, bf16[32,1,24,2048]{3,2,1,0:T(8,128)(2,1)} %bitcast.129), kind=kLoop, calls=%fused_computation.6 | loop fusion | flops 3145728 | bytes 12582912 | tf_op jit(solution)/shard_map/stack | solution.py:124
  335.9 7.5 %all-to-all-start.2 = ((bf16[32,2,24,2048]{3,2,1,0:T(8,128)(2,1)}), bf16[32,2,24,2048]{3,2,1,0:T(8,128)(2,1)}, u32[]{:S(2)}, u32[]{:S(2)}) async-start(bf16[32,2,24,2048]{3,2,1,0:T(8,128)(2,1)} %pad_maximum_fusion), calls=%async_computation.2 | async-start | bytes 12582912 | tf_op jit(solution)/shard_map/all_to_all | solution.py:126
  343.6 83.2 %all-to-all-done.2 = bf16[32,2,24,2048]{3,2,1,0:T(8,128)(2,1)} async-done(((bf16[32,2,24,2048]{3,2,1,0:T(8,128)(2,1)}), bf16[32,2,24,2048]{3,2,1,0:T(8,128)(2,1)}, u32[]{:S(2)}, u32[]{:S(2)}) %all-to-all-start.2) | async-done | bytes 6291488 | tf_op jit(solution)/shard_map/all_to_all | solution.py:126
  426.7 12.8 %gather_fusion = bf16[1024,2048]{1,0:T(8,128)(2,1)} fusion(bf16[1536,2048]{1,0:T(8,128)(2,1)} %bitcast.33, s32[1024]{0:T(1024)S(1)} %broadcast_clamp_fusion), kind=kCustom, calls=%fused_computation | custom fusion | bytes 8392704 | tf_op jit(solution)/shard_map/gather | solution.py:128
  439.5 3.4 fusion.4
  444.1 24.1 %reduce-scatter.2.cloned.1.call-done = bf16[128,512]{1,0:T(8,128)(2,1)} async-done(((bf16[128,2048]{1,0:T(8,128)(2,1)}), bf16[128,512]{1,0:T(8,128)(2,1)}) %reduce-scatter.2.cloned.1.call-update) | async-done | bytes 131088 | tf_op jit(solution)/shard_map/reduce_scatter | solution.py:130
  (71 shorter events, 23.4 us)
Async XLA Ops:
  6.5 161.7 %copy-start = (bf16[512,2048]{1,0:T(8,128)(2,1)S(1)}, bf16[512,2048]{1,0:T(8,128)(2,1)}, u32[]{:S(2)}) copy-start(bf16[512,2048]{1,0:T(8,128)(2,1)} %param.19) | copy-start | bytes 6291460
  14.3 123.0 %all-to-all-start = ((bf16[2,32,128,512]{3,2,0,1:T(8,128)(2,1)}), bf16[2,32,128,512]{3,2,0,1:T(8,128)(2,1)}, u32[]{:S(2)}, u32[]{:S(2)}) async-start(bf16[2,32,128,512]{3,2,0,1:T(8,128)(2,1)} %copy.39), calls=%async_computation | async-start | bytes 16777216 | tf_op jit(solution)/shard_map/all_to_all | solution.py:66
  25.8 187.8 %all-gather.3.cloned.1.call-start = ((), (), s32[]{:S(2)}) async-start(), calls=%async_computation.5 | async-start | bytes 2621440 | tf_op jit(solution)/shard_map/all_gather | solution.py:97
  29.8 8.0 %copy-start.11 = (s32[32]{0:T(128)S(1)}, s32[32]{0:T(128)}, u32[]{:S(2)}) copy-start(s32[32]{0:T(128)} %param.21) | copy-start | bytes 388
  29.8 9.9 %copy-start.2 = (bf16[1,128,2048]{2,1,0:T(8,128)(2,1)S(1)}, bf16[1,128,2048]{2,1,0:T(8,128)(2,1)}, u32[]{:S(2)}) copy-start(bf16[1,128,2048]{2,1,0:T(8,128)(2,1)} %param.14) | copy-start | bytes 1572868
  29.8 10.4 %copy-start.6 = (f32[2048]{0:T(1024)S(1)}, f32[2048]{0:T(1024)}, u32[]{:S(2)}) copy-start(f32[2048]{0:T(1024)} %param.15) | copy-start | bytes 24580
  160.8 2.2 copy-start.3
  165.5 4.1 copy-start.7
  169.5 47.3 %copy-start.8 = (f32[2048]{0:T(1024)S(1)}, f32[2048]{0:T(1024)}, u32[]{:S(2)}) copy-start(f32[2048]{0:T(1024)} %param.22) | copy-start | bytes 24580
  310.0 2.8 copy-start.10
  311.1 1.7 copy-start.5
  311.1 2.7 copy-start.4
  335.9 7.5 %copy-start.9 = (f32[1,128,8]{1,2,0:T(8,128)S(1)}, f32[1,128,8]{1,2,0:T(8,128)}, u32[]{:S(2)}) copy-start(f32[1,128,8]{1,2,0:T(8,128)} %param.24) | copy-start | bytes 12292
  335.9 90.8 %all-to-all-start.2 = ((bf16[32,2,24,2048]{3,2,1,0:T(8,128)(2,1)}), bf16[32,2,24,2048]{3,2,1,0:T(8,128)(2,1)}, u32[]{:S(2)}, u32[]{:S(2)}) async-start(bf16[32,2,24,2048]{3,2,1,0:T(8,128)(2,1)} %pad_maximum_fusion), calls=%async_computation.2 | async-start | bytes 12582912 | tf_op jit(solution)/shard_map/all_to_all | solution.py:126
  343.3 124.8 %reduce-scatter.2.cloned.1.call-start = ((), (), s32[]{:S(2)}) async-start(), calls=%async_computation.4 | async-start | bytes 655360 | tf_op jit(solution)/shard_map/reduce_scatter | solution.py:130
  426.7 43.1 %copy-start.1 = (bf16[512,2048]{1,0:T(8,128)(2,1)S(1)}, bf16[512,2048]{1,0:T(8,128)(2,1)}, u32[]{:S(2)}) copy-start(bf16[512,2048]{1,0:T(8,128)(2,1)} %param.19) | copy-start | bytes 6291460
Sparse Core Ops, SparseCore 0:
  169.6 43.8 all-gather.2
  444.2 23.9 reduce-scatter.1
